TPU v7x, 32 devices: a whole 2x2x4 slice. The times are simulated.
32 devices in a mesh: seq: 16 (over z, y, x), tp: 2 (over core).
Axes of the slice: x: 2, y: 2, z: 4, core: 2. Of those that a mesh axis runs over, the one named last changes fastest.
Arguments:
- node_features: bfloat16 [8192, 1024], P('seq'), may hold values from -16 to 16
- cluster_ids: int32 [8192], P('seq'), may hold values from 0 to 31
- neighbors: int32 [16, 3], replicated, may hold values from 0 to 15, as said below
- qkv_weight: bfloat16 [1024, 3, 1024], P(None, None, 'tp'), may hold values from -0.1875 to 0.1875
- out_weight: bfloat16 [1024, 1024], P('tp'), may hold values from -0.1875 to 0.1875
- virtual_gain: float32 [1024], replicated, may hold values from 0.1 to 1.9
Outputs:
- layer_output: bfloat16 [8192, 1024], P(('seq', 'tp'))
- virtual_tokens: bfloat16 [32, 1024], P('seq')
Inputs may be any that keep to these rules, and one draw needn't show every extreme that they name: `neighbors`: each row names three distinct blocks, none of them the row's own block, all in the same aligned run of 8 blocks as the row's block.
All inputs are finite; a program needn't handle non-finite values.
Results may differ from a plain program's by a relative error of at most 0.012.
The roundings to bfloat16 on the way count: a program that leaves them out, or rounds other values in their place, can miss the bound.
Values may be sent and summed in bfloat16 or wider, within the bound.
A program may use at most 128 MiB of HBM per device.

v0:
```python
import functools
import math

import jax
import jax.numpy as jnp
from jax import lax
from jax.experimental import pallas as pl
from jax.experimental.pallas import tpu as pltpu
from jax.sharding import PartitionSpec as P

VIRT_DEV = 2
LANES = 128

epsilon = 1e-06
sharpness = 2.5

MESH = pl.DeviceIdType.MESH
F32 = jnp.float32
BF16 = jnp.bfloat16


def flip(index, offset, size):
    out = index * 0
    bit = 1
    while bit < size:
        own = index // bit % 2
        out = out + bit * ((1 - own) if offset & bit else own)
        bit *= 2
    return out


def flip_traced(index, offset, size):
    out = index * 0
    bit = 1
    while bit < size:
        own = index // bit % 2
        other = offset // bit % 2
        out = out + bit * ((own + other) % 2)
        bit *= 2
    return out


def kernel(
    n_seq, group, head,
    x_hbm, ids_ref, nb_ref, w_hbm, ow_hbm, gain_ref,
    out_ref, tok_ref,
    x_ref, w_q, w_kv, ow_ref,
    kv_send, kv_recv, q_send, q_recv, vx, vkx, vvx,
    pool_send, pool_recv, tok_send, tok_recv, vall, ow_other, ret_send, ret_recv,
    in_sem, unit_sem,
    a_ssem, a_rsem, q_ssem, q_rsem, p_ssem, p_rsem, t_ssem, t_rsem, o_ssem, o_rsem, r_ssem, r_rsem,
):
    seq = lax.axis_index("seq")
    core = lax.axis_index("tp")
    g = seq % group
    base = seq - g
    rows, width = x_ref.shape
    half = rows // 2
    quarter = rows // 4
    virt = VIRT_DEV * n_seq
    scale = sharpness / math.sqrt(head)
    units = group // 2

    barrier = pltpu.get_barrier_semaphore()

    def loop(count, body):
        def run(step, carry):
            body(step)
            return carry

        lax.fori_loop(0, count, run, 0)

    loop(
        n_seq - 1,
        lambda step: pl.semaphore_signal(
            barrier, inc=1, device_id=((seq + 1 + step) % n_seq, core), device_id_type=MESH
        ),
    )
    loop(
        group,
        lambda step: pl.semaphore_signal(
            barrier, inc=1, device_id=(base + step, 1 - core), device_id_type=MESH
        ),
    )

    x_load = pltpu.make_async_copy(x_hbm, x_ref, in_sem.at[0])
    x_load.start()
    unit_loads = []
    for u in range(units):
        pair = flip(g // 2, u, units)
        cols = pl.ds(pl.multiple_of(pair * LANES, LANES), LANES)
        unit_loads.append(
            pltpu.make_async_copy(w_hbm.at[pl.ds(1, 2), :, cols], w_kv.at[u], unit_sem.at[u])
        )
        unit_loads[u].start()
    q_load = pltpu.make_async_copy(w_hbm.at[0], w_q, in_sem.at[1])
    q_load.start()
    ow_load = pltpu.make_async_copy(ow_hbm, ow_ref, in_sem.at[2])
    ow_load.start()

    lane = lax.broadcasted_iota(jnp.int32, (rows, LANES), 1)
    low = lane < head
    low_half = low[:half]
    seg_a = lax.broadcasted_iota(jnp.int32, (LANES, LANES), 0) // head
    seg_b = lax.broadcasted_iota(jnp.int32, (LANES, LANES), 1) // head
    ones_block = (seg_a == seg_b).astype(F32).astype(BF16)

    def normed(values):
        square = values * values
        hi = square.astype(BF16)
        lo = (square - hi.astype(F32)).astype(BF16)
        total = jnp.dot(hi, ones_block, preferred_element_type=F32) + jnp.dot(
            lo, ones_block, preferred_element_type=F32
        )
        return values * lax.rsqrt(total * (1.0 / head) + epsilon)

    def a_copy(o):
        peer = flip(g, o, group)
        return pltpu.make_async_remote_copy(
            src_ref=kv_send.at[peer], dst_ref=kv_recv.at[g],
            send_sem=a_ssem.at[o], recv_sem=a_rsem.at[o],
            device_id=(base + peer, core), device_id_type=MESH,
        )

    def q_copy(o, peer):
        return pltpu.make_async_remote_copy(
            src_ref=q_send.at[peer], dst_ref=q_recv.at[g],
            send_sem=q_ssem.at[o], recv_sem=q_rsem.at[o],
            device_id=(base + peer, core), device_id_type=MESH,
        )

    def p_copy(step):
        peer = (seq + 1 + step) % n_seq
        return pltpu.make_async_remote_copy(
            src_ref=pool_send.at[peer], dst_ref=pool_recv.at[step],
            send_sem=p_ssem.at[step], recv_sem=p_rsem.at[step],
            device_id=(peer, core), device_id_type=MESH,
        )

    def t_copy(step):
        peer = (seq + 1 + step) % n_seq
        return pltpu.make_async_remote_copy(
            src_ref=tok_send, dst_ref=tok_recv.at[seq],
            send_sem=t_ssem.at[step], recv_sem=t_rsem.at[step],
            device_id=(peer, core), device_id_type=MESH,
        )

    o_copy = pltpu.make_async_remote_copy(
        src_ref=ow_ref, dst_ref=ow_other, send_sem=o_ssem, recv_sem=o_rsem,
        device_id=(seq, 1 - core), device_id_type=MESH,
    )

    x_load.wait()
    member = (
        lax.broadcasted_iota(jnp.int32, (virt, rows), 0) == jnp.broadcast_to(ids_ref[...], (virt, rows))
    ).astype(F32).astype(BF16)
    pool = jnp.dot(member, x_ref[...], preferred_element_type=F32)
    for p in range(n_seq):
        pool_send[p] = pool[VIRT_DEV * p : VIRT_DEV * (p + 1), :]

    def project(u):
        pair = flip(g // 2, u, units)
        unit_loads[u].wait()
        weights = jnp.concatenate([w_kv[u, 0], w_kv[u, 1]], axis=1)
        kv = jnp.dot(x_ref[...], weights, preferred_element_type=F32).astype(BF16).astype(F32)
        k, v = normed(kv[:, :LANES]), kv[:, LANES:]
        kv_send[pair * 2] = jnp.where(low, k, pltpu.roll(v, head, 1)).astype(BF16)
        kv_send[pair * 2 + 1] = jnp.where(low, pltpu.roll(k, head, 1), v).astype(BF16)

    early = [1 << bit for bit in range(group.bit_length() - 1)]
    if group > 2:
        early.append(group - 1)
    late = [o for o in range(group - 1, 0, -1) if o not in early]
    done = set()
    for o in early:
        if o // 2 not in done:
            project(o // 2)
        if not done:
            pl.semaphore_wait(barrier, n_seq - 1 + group)
            loop(n_seq - 1, lambda step: p_copy(step).start())
        done.add(o // 2)
        a_copy(o).start()
    for u in range(units):
        if u not in done:
            project(u)

    for o in late:
        a_copy(o).start()
    loop(n_seq - 1, lambda step: p_copy(step).wait())
    pool_recv[n_seq - 1] = pool_send[seq]

    def add(step, total):
        return total + pool_recv[(seq + n_seq - 1 - step) % n_seq]

    pooled = lax.fori_loop(0, n_seq, add, jnp.zeros((VIRT_DEV, width), F32))
    tokens = pooled * lax.rsqrt(jnp.mean(pooled * pooled, axis=-1, keepdims=True) + epsilon)
    tokens = (tokens * gain_ref[...]).astype(BF16)
    tok_ref[...] = tokens
    tok_send[...] = tokens.astype(F32)
    tok_recv[seq] = tokens.astype(F32)
    loop(n_seq - 1, lambda step: t_copy(step).start())
    q_load.wait()
    for i in range(units):
        q = jnp.dot(
            x_ref[...], w_q[:, i * LANES : (i + 1) * LANES], preferred_element_type=F32
        ).astype(BF16).astype(F32)
        q = normed(q) * scale
        top, bottom = q[:half], q[half:]
        q_send[2 * i] = jnp.where(low_half, top, pltpu.roll(bottom, head, 1)).astype(BF16)
        q_send[2 * i + 1] = jnp.where(low_half, pltpu.roll(top, head, 1), bottom).astype(BF16)

    for o in range(group - 1, 0, -1):
        q_copy(o, flip(g, o, group)).start()
    ow_load.wait()
    o_copy.start()

    def spread(block):
        vx[block] = jnp.where(low, 1.0, kv_recv[block].astype(F32)).astype(BF16)

    kv_recv[g] = kv_send[g]
    q_recv[g] = q_send[g]
    spread(g)
    for o in early + late:
        a_copy(o).wait()
        spread(flip(g, o, group))

    def r_copy(o, block, e):
        to_core = (core + e) % 2
        return pltpu.make_async_remote_copy(
            src_ref=ret_send.at[block, to_core], dst_ref=ret_recv.at[core, g],
            send_sem=r_ssem.at[e, o], recv_sem=r_rsem.at[e, o],
            device_id=(base + block, to_core), device_id_type=MESH,
        )

    def piece(query, key_rows, value_rows):
        scores = lax.dot_general(
            query, key_rows, (((1,), (1,)), ((), ())), preferred_element_type=F32
        )
        raised = jnp.exp(scores).astype(BF16)
        return jnp.dot(raised, value_rows, preferred_element_type=F32)

    def receive_virtual():
        loop(n_seq - 1, lambda step: t_copy(step).wait())
        for p in range(n_seq):
            vall[VIRT_DEV * p : VIRT_DEV * (p + 1), :] = tok_recv[p]
        weights = jnp.concatenate([w_kv[0, 0], w_kv[0, 1]], axis=1)
        pairs = jnp.dot(vall[...].astype(BF16), weights, preferred_element_type=F32)
        pairs = pairs.astype(BF16).astype(F32)
        vk, vv = normed(pairs[:, :LANES]), pairs[:, LANES:]
        odd = jnp.broadcast_to(g % 2, (virt, LANES)) == 1
        vlow = lax.broadcasted_iota(jnp.int32, (virt, LANES), 1) < head
        vk = jnp.where(odd, pltpu.roll(vk, head, 1), vk)
        vkx[...] = jnp.where(vlow, vk, 0.0).astype(BF16)
        vv = jnp.where(odd, vv, pltpu.roll(vv, head, 1))
        vvx[...] = jnp.where(vlow, 1.0, vv).astype(BF16)

    def one_block(o):
        o = (group - o) % group
        block = flip_traced(g, o, group)

        @pl.when(o != 0)
        def _():
            q_copy(o, block).wait()

        packed = q_recv[block].astype(F32)
        query = jnp.concatenate(
            [
                jnp.where(low_half, packed, 0.0),
                jnp.where(low_half, pltpu.roll(packed, head, 1), 0.0),
            ],
            axis=0,
        ).astype(BF16)
        total = piece(query, kv_recv[block], vx[block])
        for j in range(nb_ref.shape[0]):
            other = nb_ref[j, base + block] % group
            total = total + piece(query, kv_recv[other], vx[other])

        pl.when(o == 0)(receive_virtual)

        total = total + piece(query, vkx[...], vvx[...])
        mixed = total / pltpu.roll(total, head, 1)
        shifted = pltpu.roll(mixed, head, 1)
        for t in range(2):
            first = shifted[t * half : t * half + quarter]
            second = mixed[t * half + quarter : (t + 1) * half]
            ret_send[block, t] = jnp.where(low[:quarter], first, second).astype(BF16)

        r_copy(o, block, 1).start()

        @pl.when(o != 0)
        def _():
            r_copy(o, block, 0).start()

    loop(group, one_block)
    ret_recv[core, g] = ret_send[g, core]

    o_copy.wait()
    for o in range(group):
        for e in range(2):
            if o or e:
                r_copy(o, flip(g, o, group), e).wait()

    lowq = low[:quarter]

    def gathered(side):
        tops, bottoms = [], []
        for i in range(units):
            a = ret_recv[side, 2 * i].astype(F32)
            b = ret_recv[side, 2 * i + 1].astype(F32)
            tops.append(jnp.where(lowq, a, pltpu.roll(b, head, 1)).astype(BF16))
            bottoms.append(jnp.where(lowq, pltpu.roll(a, head, 1), b).astype(BF16))
        return jnp.concatenate(
            [jnp.concatenate(tops, axis=1), jnp.concatenate(bottoms, axis=1)], axis=0
        )

    result = jnp.dot(gathered(core), ow_ref[...], preferred_element_type=F32)
    result = result + jnp.dot(gathered(1 - core), ow_other[...], preferred_element_type=F32)
    out_ref[...] = result.astype(BF16)


def solution(mesh):
    n_seq = mesh.shape["seq"]

    def body(node_features, cluster_ids, neighbors, qkv_weight, out_weight, virtual_gain):
        rows, width = node_features.shape
        local = qkv_weight.shape[2]
        head = LANES // 2
        group = local // head
        virt = VIRT_DEV * n_seq
        vmem = pl.BlockSpec(memory_space=pltpu.VMEM)
        any_ = pl.BlockSpec(memory_space=pl.ANY)
        dma = pltpu.SemaphoreType.DMA
        return pl.pallas_call(
            functools.partial(kernel, n_seq, group, head),
            out_shape=(
                jax.ShapeDtypeStruct((rows // 2, width), BF16),
                jax.ShapeDtypeStruct((VIRT_DEV, width), BF16),
            ),
            in_specs=[any_, vmem, pl.BlockSpec(memory_space=pltpu.SMEM), any_, any_, vmem],
            out_specs=(vmem, vmem),
            scratch_shapes=[
                pltpu.VMEM((rows, width), BF16),
                pltpu.VMEM((width, local), BF16),
                pltpu.VMEM((group // 2, 2, width, LANES), BF16),
                pltpu.VMEM((local, width), BF16),
                pltpu.VMEM((group, rows, LANES), BF16),
                pltpu.VMEM((group, rows, LANES), BF16),
                pltpu.VMEM((group, rows // 2, LANES), BF16),
                pltpu.VMEM((group, rows // 2, LANES), BF16),
                pltpu.VMEM((group, rows, LANES), BF16),
                pltpu.VMEM((virt, LANES), BF16),
                pltpu.VMEM((virt, LANES), BF16),
                pltpu.VMEM((n_seq, VIRT_DEV, width), F32),
                pltpu.VMEM((n_seq, VIRT_DEV, width), F32),
                pltpu.VMEM((VIRT_DEV, width), F32),
                pltpu.VMEM((n_seq, VIRT_DEV, width), F32),
                pltpu.VMEM((virt, width), F32),
                pltpu.VMEM((local, width), BF16),
                pltpu.VMEM((group, 2, rows // 4, LANES), BF16),
                pltpu.VMEM((2, group, rows // 4, LANES), BF16),
                dma((3,)),
                dma((group // 2,)),
                dma((group,)),
                dma((group,)),
                dma((group,)),
                dma((group,)),
                dma((n_seq,)),
                dma((n_seq,)),
                dma((n_seq,)),
                dma((n_seq,)),
                dma,
                dma,
                dma((2, group)),
                dma((2, group)),
            ],
            compiler_params=pltpu.CompilerParams(
                collective_id=0, has_side_effects=True, vmem_limit_bytes=60 * 1024 * 1024
            ),
        )(
            node_features,
            cluster_ids.reshape(1, rows),
            neighbors.T,
            qkv_weight.transpose(1, 0, 2),
            out_weight,
            virtual_gain.reshape(1, width),
        )

    return jax.shard_map(
        body,
        mesh=mesh,
        in_specs=(P("seq", None), P("seq"), P(), P(None, None, "tp"), P("tp", None), P()),
        out_specs=(P(("seq", "tp"), None), P("seq", None)),
        check_vma=False,
    )
```

profile of v0, /device:TPU:0, one launch (start us, length us, event | category | flops | bytes accessed | tf_op | source)
XLA Modules:
  0.0 53.5 jit_solution(7952951053966939312)
XLA Ops:
  0.6 49.8 %shard_map.77 = (bf16[256,1024]{1,0:T(8,128)(2,1)}, bf16[2,1024]{1,0:T(2,128)(2,1)}) custom-call(bf16[512,1024]{1,0:T(8,128)(2,1)} %x_hbm.1, s32[1,512]{1,0:T(1,128)} %bitcast.6, s32[3,16]{1,0:T(4,128)} %bitcast.7, bf16[3,1024,512]{2,1,0:T(8,128)(2,1)} %bitcast.4, bf16[512,1024]{1,0:T(8,128)(2,1)} %ow_hbm.1, f32[1,1024]{1,0:T(1,128)} %bitcast.5), custom_call_target="tpu_custom_call" | custom-call | tf_op jit(solution)/shard_map/pallas_call | solution.py:333
  50.4 1.9 %copy.10 = bf16[256,1024]{1,0:T(8,128)(2,1)} copy(bf16[256,1024]{1,0:T(8,128)(2,1)} %get-tuple-element.4) | data formatting | bytes 1048576
  52.3 1.3 %copy.11 = bf16[2,1024]{1,0:T(2,128)(2,1)} copy(bf16[2,1024]{1,0:T(2,128)(2,1)} %get-tuple-element.5) | data formatting | bytes 8192
where the time goes:
time: 53.8 us; the launch traced here: 53.5 us
  Pallas kernels  49.8 us (93%)
  local copies, waits for them, and re-layouts  3.14 us (6%)
  between operations  0.64 us (1%)
    pallas_call x1, Pallas kernels, body(): pl.pallas_call(functools.partial(kernel, n_seq, group, head), out_shape=(...  49.8 us
    unnamed x2, local copies, waits for them, and re-layouts  3.14 us

commit v1 on v0

--- a/solution.py
+++ b/solution.py
@@ -186,19 +186,6 @@
 
     for o in late:
         a_copy(o).start()
-    loop(n_seq - 1, lambda step: p_copy(step).wait())
-    pool_recv[n_seq - 1] = pool_send[seq]
-
-    def add(step, total):
-        return total + pool_recv[(seq + n_seq - 1 - step) % n_seq]
-
-    pooled = lax.fori_loop(0, n_seq, add, jnp.zeros((VIRT_DEV, width), F32))
-    tokens = pooled * lax.rsqrt(jnp.mean(pooled * pooled, axis=-1, keepdims=True) + epsilon)
-    tokens = (tokens * gain_ref[...]).astype(BF16)
-    tok_ref[...] = tokens
-    tok_send[...] = tokens.astype(F32)
-    tok_recv[seq] = tokens.astype(F32)
-    loop(n_seq - 1, lambda step: t_copy(step).start())
     q_load.wait()
     for i in range(units):
         q = jnp.dot(
@@ -209,6 +196,19 @@
         q_send[2 * i] = jnp.where(low_half, top, pltpu.roll(bottom, head, 1)).astype(BF16)
         q_send[2 * i + 1] = jnp.where(low_half, pltpu.roll(top, head, 1), bottom).astype(BF16)
 
+    loop(n_seq - 1, lambda step: p_copy(step).wait())
+    pool_recv[n_seq - 1] = pool_send[seq]
+
+    def add(step, total):
+        return total + pool_recv[(seq + n_seq - 1 - step) % n_seq]
+
+    pooled = lax.fori_loop(0, n_seq, add, jnp.zeros((VIRT_DEV, width), F32))
+    tokens = pooled * lax.rsqrt(jnp.mean(pooled * pooled, axis=-1, keepdims=True) + epsilon)
+    tokens = (tokens * gain_ref[...]).astype(BF16)
+    tok_ref[...] = tokens
+    tok_send[...] = tokens.astype(F32)
+    tok_recv[seq] = tokens.astype(F32)
+    loop(n_seq - 1, lambda step: t_copy(step).start())
     for o in range(group - 1, 0, -1):
         q_copy(o, flip(g, o, group)).start()
     ow_load.wait()
@@ -275,8 +275,6 @@
             other = nb_ref[j, base + block] % group
             total = total + piece(query, kv_recv[other], vx[other])
 
-        pl.when(o == 0)(receive_virtual)
-
         total = total + piece(query, vkx[...], vvx[...])
         mixed = total / pltpu.roll(total, head, 1)
         shifted = pltpu.roll(mixed, head, 1)
@@ -291,6 +289,7 @@
         def _():
             r_copy(o, block, 0).start()
 
+    receive_virtual()
     loop(group, one_block)
     ret_recv[core, g] = ret_send[g, core]
 

time: 53.8 us -> 51 us (0.948)
  Pallas kernels: 49.8 us -> 47 us
    pallas_call x1, Pallas kernels: 49.8 us -> 47 us  [body(): pl.pallas_call(functools.partial(kernel, n_seq, group, head), out_shape=(...]
where the time goes in v1:
time: 51 us; the launch traced here: 50.8 us
  Pallas kernels  47 us (92%)
  local copies, waits for them, and re-layouts  3.14 us (6%)
  between operations  0.64 us (1%)
    pallas_call x1, Pallas kernels, body(): pl.pallas_call(functools.partial(kernel, n_seq, group, head), out_shape=(...  47 us
    unnamed x2, local copies, waits for them, and re-layouts  3.14 us

profile of v1, /device:TPU:0, one launch (start us, length us, event | category | flops | bytes accessed | tf_op | source)
XLA Modules:
  0.0 50.8 jit_solution(3573460700680276301)
XLA Ops:
  0.6 47.0 %shard_map.77 = (bf16[256,1024]{1,0:T(8,128)(2,1)}, bf16[2,1024]{1,0:T(2,128)(2,1)}) custom-call(bf16[512,1024]{1,0:T(8,128)(2,1)} %x_hbm.1, s32[1,512]{1,0:T(1,128)} %bitcast.6, s32[3,16]{1,0:T(4,128)} %bitcast.7, bf16[3,1024,512]{2,1,0:T(8,128)(2,1)} %bitcast.4, bf16[512,1024]{1,0:T(8,128)(2,1)} %ow_hbm.1, f32[1,1024]{1,0:T(1,128)} %bitcast.5), custom_call_target="tpu_custom_call" | custom-call | tf_op jit(solution)/shard_map/pallas_call | solution.py:332
  47.6 1.9 %copy.10 = bf16[256,1024]{1,0:T(8,128)(2,1)} copy(bf16[256,1024]{1,0:T(8,128)(2,1)} %get-tuple-element.4) | data formatting | bytes 1048576
  49.5 1.3 %copy.11 = bf16[2,1024]{1,0:T(2,128)(2,1)} copy(bf16[2,1024]{1,0:T(2,128)(2,1)} %get-tuple-element.5) | data formatting | bytes 8192
